TPU v7x, 32 devices: a whole 2x2x4 slice. The times are simulated.
32 devices in a mesh: occ: 8 (over z, x), aux: 4 (over y, core).
Axes of the slice: x: 2, y: 2, z: 4, core: 2. Of those that a mesh axis runs over, the one named last changes fastest.
Arguments:
- half_integrals: bfloat16 [8, 1024, 1024], P(None, 'aux'), may hold values from -1 to 1
- vir_coef: bfloat16 [1024, 768], P(None, 'occ'), may hold values from -0.1875 to 0.1875
- occ_energy: float32 [8], replicated, may hold values from -3 to -0.3
- vir_energy: float32 [768], replicated, may hold values from 0.1 to 2
Outputs:
- three_index: float32 [1024, 8, 768], P('aux', 'occ')
- vir_density: float32 [768, 768], P(('occ', 'aux'))
All inputs are finite; a program needn't handle non-finite values.
Results may differ from a plain program's by a relative error of at most 0.0006.
The roundings to bfloat16 on the way count: a program that leaves them out, or rounds other values in their place, can miss the bound.
Values may be sent and summed in bfloat16 or wider, within the bound.
A program may use at most 64 MiB of HBM per device.

v0:
```python
import jax
import jax.numpy as jnp
from jax import lax
from jax.sharding import PartitionSpec as P


def from_behind(array, axis, by):
    size = lax.axis_size(axis)
    return lax.ppermute(array, axis, [(i, (i + by) % size) for i in range(size)])


def amplitudes(own_block, own_energy, arrival, arrival_energy, vir_energy, slice_energy):
    coulomb = jnp.einsum("jbp,iap->ijba", arrival, own_block, preferred_element_type=jnp.float32)
    denominator = (
        own_energy[:, None, None, None]
        + arrival_energy[None, :, None, None]
        - slice_energy[None, None, :, None]
        - vir_energy[None, None, None, :]
    )
    return (coulomb / denominator).astype(jnp.bfloat16)


def per_device(half_integrals, vir_coef, occ_energy, vir_energy):
    partial_block = jnp.einsum(
        "ipm,ma->iap", half_integrals, vir_coef, preferred_element_type=jnp.float32
    ).astype(jnp.bfloat16)
    local_block = lax.all_to_all(partial_block, "occ", split_axis=0, concat_axis=1, tiled=True)
    own_block = lax.all_gather(local_block, "aux", axis=2, tiled=True)
    cycle_size = lax.axis_size("occ")
    aux_size = lax.axis_size("aux")
    block_rows, virtuals, aux_total = own_block.shape
    slice_width = virtuals // aux_size
    first_virtual = lax.axis_index("aux") * slice_width
    visitor = lax.dynamic_slice_in_dim(own_block, first_virtual, slice_width, 1)
    slice_energy = lax.dynamic_slice_in_dim(vir_energy, first_virtual, slice_width, 0)
    my_index = lax.axis_index("occ")

    def energy_of(anchor):
        return lax.dynamic_slice_in_dim(occ_energy, anchor % cycle_size * block_rows, block_rows, 0)

    own_energy = energy_of(my_index)
    amp_stack = jnp.zeros((cycle_size, block_rows, block_rows, slice_width, virtuals), jnp.bfloat16)
    store_buffer = jnp.zeros((cycle_size, block_rows, slice_width, aux_total), jnp.bfloat16)

    def absorb(ledger, position, arrival, arrival_energy):
        stacked, keeper = ledger
        amplitude = amplitudes(
            own_block, own_energy, arrival, arrival_energy, vir_energy, slice_energy
        )
        stacked = lax.dynamic_update_index_in_dim(stacked, amplitude, position, 0)
        keeper = lax.dynamic_update_index_in_dim(keeper, arrival, position, 0)
        return (stacked, keeper)

    ledger = absorb((amp_stack, store_buffer), 0, visitor, own_energy)

    def one_turn(turn_index, payload):
        ledger, arrival = payload
        arrival = from_behind(arrival, "occ", 1)
        ledger = absorb(ledger, turn_index, arrival, energy_of(my_index - turn_index))
        return (ledger, arrival)

    ledger, arrival = lax.fori_loop(1, cycle_size, one_turn, (ledger, visitor))
    amp_stack, store_buffer = ledger
    three_index = lax.psum_scatter(
        jnp.einsum("sijba,sjbp->pia", amp_stack, store_buffer, preferred_element_type=jnp.float32),
        "aux",
        scatter_dimension=0,
        tiled=True,
    )
    vir_sum = jnp.einsum(
        "sijca,sijcd->ad", amp_stack, amp_stack, preferred_element_type=jnp.float32
    )
    vir_rows = lax.psum_scatter(vir_sum, ("occ", "aux"), scatter_dimension=0, tiled=True)
    return (three_index, vir_rows / (block_rows * cycle_size * virtuals))


def solution(mesh):
    return jax.shard_map(
        per_device,
        mesh=mesh,
        in_specs=(P(None, "aux", None), P(None, "occ"), P(), P()),
        out_specs=(P("aux", "occ", None), P(("occ", "aux"), None)),
        check_vma=False,
    )
```

profile of v0, /device:TPU:0, one launch (start us, length us, event | category | flops | bytes accessed | tf_op | source)
XLA Modules:
  0.0 311.1 jit_solution(6742861085292702216)
XLA Ops:
  7.2 0.0 copy-start
  7.2 0.0 copy-start.4
  7.2 0.0 copy-start.3
  7.2 0.0 all-gather.2.cloned.1.call-start
  7.2 0.9 copy-done
  8.1 3.6 %fusion.36 = bf16[8,96,256]{2,1,0:T(8,128)(2,1)S(1)} fusion(bf16[8,256,1024]{2,1,0:T(8,128)(2,1)} %param.6, bf16[1024,96]{0,1:T(8,128)(2,1)S(1)} %copy-done), kind=kOutput, calls=%fused_computation.21 | convolution fusion | flops 402849792 | bytes 4784128 | tf_op jit(solution)/shard_map/ipm,ma->iap/dot_general | solution.py:24
  11.7 19.2 %all_to_all.12 = bf16[8,96,256]{2,1,0:T(8,128)(2,1)} all-to-all(bf16[8,96,256]{2,1,0:T(8,128)(2,1)S(1)} %fusion.36), channel_id=1, replica_groups=mesh['occ'=8,'aux'=4] {'occ'}, dimensions={0} | all-to-all | bytes 786432 | tf_op jit(solution)/shard_map/all_to_all | solution.py:27
  30.9 0.0 all-gather.2.cloned.1.call-update
  31.0 0.0 reduce-scatter.5.cloned.1.call-start
  31.0 0.0 copy-done.4
  31.0 0.6 dynamic_slice.23
  32.7 0.1 broadcast_subtract_fusion.1
  32.8 16.9 %all-gather.2.cloned.1.call-done = bf16[1,768,1024]{2,1,0:T(8,128)(2,1)} async-done(((bf16[1,768,256]{2,1,0:T(8,128)(2,1)}), bf16[1,768,1024]{2,1,0:T(8,128)(2,1)}) %all-gather.2.cloned.1.call-update) | async-done | bytes 1572880 | tf_op jit(solution)/shard_map/all_gather | solution.py:28
  49.6 1.0 constant_dynamic-slice_fusion
  50.7 2.1 fusion.43
  52.8 0.2 dynamic_update_slice.34
  52.9 1.0 fusion.49
  54.0 2.0 dynamic_update_slice.35
  56.0 102.9 %while.21 = (s32[]{:T(128)}, bf16[8,1,1,192,768]{4,3,2,1,0:T(8,128)(2,1)S(1)}, bf16[8,1,192,1024]{3,2,1,0:T(8,128)(2,1)}, bf16[1,192,1024]{2,1,0:T(8,128)(2,1)S(...) while((s32[]{:T(128)}, ...), condition=%wide.region_1.2_spmd, body=%wide.region_0.1_spmd.sunk | while | flops 302432480 | bytes 5413790 | solution.py:62
  56.0 1.5 collective-permute-start
  57.4 0.7 dynamic_slice.30
  59.4 10.6 %collective-permute-done = bf16[1,192,1024]{2,1,0:T(8,128)(2,1)S(1)} collective-permute-done((bf16[1,192,1024]{2,1,0:T(8,128)(2,1)S(1)}, bf16[1,192,1024]{2,1,0:T(8,128)(2,1)S(1)}, u32[]{:S(2)}, u32[]{:S(2)}) %collective-permute-start) | collective-permute-done | bytes 393248 | tf_op jit(solution)/shard_map/while/body/eval_jaxpr/ppermute | solution.py:9
  70.0 0.8 bitcast_dynamic-update-slice_fusion.2
  70.7 2.1 fusion.55
  72.8 0.1 collective-permute-start
  72.9 0.7 dynamic_slice.30
  74.9 11.2 %collective-permute-done = bf16[1,192,1024]{2,1,0:T(8,128)(2,1)S(1)} collective-permute-done((bf16[1,192,1024]{2,1,0:T(8,128)(2,1)S(1)}, bf16[1,192,1024]{2,1,0:T(8,128)(2,1)S(1)}, u32[]{:S(2)}, u32[]{:S(2)}) %collective-permute-start) | collective-permute-done | bytes 393248 | tf_op jit(solution)/shard_map/while/body/eval_jaxpr/ppermute | solution.py:9
  86.0 0.8 bitcast_dynamic-update-slice_fusion.2
  86.8 2.1 fusion.55
  88.9 0.1 collective-permute-start
  89.0 0.7 dynamic_slice.30
  90.9 10.3 %collective-permute-done = bf16[1,192,1024]{2,1,0:T(8,128)(2,1)S(1)} collective-permute-done((bf16[1,192,1024]{2,1,0:T(8,128)(2,1)S(1)}, bf16[1,192,1024]{2,1,0:T(8,128)(2,1)S(1)}, u32[]{:S(2)}, u32[]{:S(2)}) %collective-permute-start) | collective-permute-done | bytes 393248 | tf_op jit(solution)/shard_map/while/body/eval_jaxpr/ppermute | solution.py:9
  101.3 0.8 bitcast_dynamic-update-slice_fusion.2
  102.1 2.1 fusion.55
  104.2 0.1 collective-permute-start
  104.3 0.7 dynamic_slice.30
  106.2 9.4 %collective-permute-done = bf16[1,192,1024]{2,1,0:T(8,128)(2,1)S(1)} collective-permute-done((bf16[1,192,1024]{2,1,0:T(8,128)(2,1)S(1)}, bf16[1,192,1024]{2,1,0:T(8,128)(2,1)S(1)}, u32[]{:S(2)}, u32[]{:S(2)}) %collective-permute-start) | collective-permute-done | bytes 393248 | tf_op jit(solution)/shard_map/while/body/eval_jaxpr/ppermute | solution.py:9
  115.6 0.8 bitcast_dynamic-update-slice_fusion.2
  116.4 2.1 fusion.55
  118.5 0.1 collective-permute-start
  118.6 0.7 dynamic_slice.30
  120.5 8.6 %collective-permute-done = bf16[1,192,1024]{2,1,0:T(8,128)(2,1)S(1)} collective-permute-done((bf16[1,192,1024]{2,1,0:T(8,128)(2,1)S(1)}, bf16[1,192,1024]{2,1,0:T(8,128)(2,1)S(1)}, u32[]{:S(2)}, u32[]{:S(2)}) %collective-permute-start) | collective-permute-done | bytes 393248 | tf_op jit(solution)/shard_map/while/body/eval_jaxpr/ppermute | solution.py:9
  129.1 0.8 bitcast_dynamic-update-slice_fusion.2
  129.9 2.1 fusion.55
  132.0 0.1 collective-permute-start
  132.1 0.7 dynamic_slice.30
  134.0 8.5 %collective-permute-done = bf16[1,192,1024]{2,1,0:T(8,128)(2,1)S(1)} collective-permute-done((bf16[1,192,1024]{2,1,0:T(8,128)(2,1)S(1)}, bf16[1,192,1024]{2,1,0:T(8,128)(2,1)S(1)}, u32[]{:S(2)}, u32[]{:S(2)}) %collective-permute-start) | collective-permute-done | bytes 393248 | tf_op jit(solution)/shard_map/while/body/eval_jaxpr/ppermute | solution.py:9
  142.6 0.8 bitcast_dynamic-update-slice_fusion.2
  143.3 2.1 fusion.55
  145.4 0.1 collective-permute-start
  145.5 0.7 dynamic_slice.30
  147.5 8.5 %collective-permute-done = bf16[1,192,1024]{2,1,0:T(8,128)(2,1)S(1)} collective-permute-done((bf16[1,192,1024]{2,1,0:T(8,128)(2,1)S(1)}, bf16[1,192,1024]{2,1,0:T(8,128)(2,1)S(1)}, u32[]{:S(2)}, u32[]{:S(2)}) %collective-permute-start) | collective-permute-done | bytes 393248 | tf_op jit(solution)/shard_map/while/body/eval_jaxpr/ppermute | solution.py:9
  156.0 0.8 bitcast_dynamic-update-slice_fusion.2
  156.8 2.1 fusion.55
  158.9 1.4 copy-done.2
  160.3 6.1 %fusion.28 = f32[768,768]{1,0:T(8,128)} fusion(bf16[8,1,1,192,768]{4,3,2,1,0:T(8,128)(2,1)} %copy-done.2), kind=kOutput, calls=%fused_computation.16 | convolution fusion | flops 1811939328 | bytes 4718592 | tf_op jit(solution)/shard_map/sijca,sijcd->ad/dot_general | solution.py:70
  166.3 0.0 reduce-scatter.5.cloned.1.call-update
  166.4 0.0 reduce-scatter.3.cloned.1.call-start
  166.4 6.0 %fusion.23 = f32[1024,1,768]{2,0,1:T(8,128)} fusion(bf16[8,1,1,192,768]{4,3,2,1,0:T(8,128)(2,1)} %copy-done.2, bf16[8,1,192,1024]{3,2,1,0:T(8,128)(2,1)S(1)} %copy-done.1), kind=kOutput, calls=%fused_computation.15 | convolution fusion | flops 2415919104 | bytes 8650752 | tf_op jit(solution)/shard_map/sijba,sjbp->pia/dot_general | solution.py:65
  172.4 0.0 reduce-scatter.3.cloned.1.call-update
  172.4 89.9 %reduce-scatter.5.cloned.1.call-done = f32[24,768]{1,0:T(8,128)} async-done(((f32[768,768]{1,0:T(8,128)}), f32[24,768]{1,0:T(8,128)}) %reduce-scatter.5.cloned.1.call-update) | async-done | bytes 73744 | tf_op jit(solution)/shard_map/reduce_scatter | solution.py:73
  262.3 1.5 broadcast_multiply_fusion
  263.9 37.9 %reduce-scatter.3.cloned.1.call-done = f32[256,1,768]{2,0,1:T(8,128)} async-done(((f32[1024,1,768]{2,0,1:T(8,128)}), f32[256,1,768]{2,0,1:T(8,128)}) %reduce-scatter.3.cloned.1.call-update) | async-done | bytes 786448 | tf_op jit(solution)/shard_map/reduce_scatter | solution.py:64
  301.7 2.8 copy.6
  (18 shorter events, 0.2 us)
Async XLA Ops:
  7.2 0.9 copy-start
  7.2 23.9 %copy-start.4 = (f32[8]{0:T(128)S(1)}, f32[8]{0:T(128)}, u32[]{:S(2)}) copy-start(f32[8]{0:T(128)} %param.8) | copy-start | bytes 100
  7.2 25.5 %copy-start.3 = (f32[768]{0:T(1024)S(1)}, f32[768]{0:T(1024)}, u32[]{:S(2)}) copy-start(f32[768]{0:T(1024)} %param.9) | copy-start | bytes 9220
  7.2 42.4 %all-gather.2.cloned.1.call-start = ((), (), s32[]{:S(2)}) async-start(), calls=%async_computation.3 | async-start | bytes 1966080 | tf_op jit(solution)/shard_map/all_gather | solution.py:28
  31.0 231.4 %reduce-scatter.5.cloned.1.call-start = ((), (), s32[]{:S(2)}) async-start(), calls=%async_computation.5 | async-start | bytes 2433024 | tf_op jit(solution)/shard_map/reduce_scatter | solution.py:73
  56.0 14.0 %collective-permute-start = (bf16[1,192,1024]{2,1,0:T(8,128)(2,1)S(1)}, bf16[1,192,1024]{2,1,0:T(8,128)(2,1)S(1)}, u32[]{:S(2)}, u32[]{:S(2)}) collective-permute-start(bf16[1,192,1024]{2,1,0:T(8,128)(2,1)S(1)} %get-tuple-element.424), channel_id=1, source_target_pairs={{0,4},{4,8},{8,12},{12,16},{16,20},{20,24},{24,28},{28,0},{1,5},{5... | collective-permute-start | bytes 1179656 | tf_op jit(solution)/shard_map/while/body/eval_jaxpr/ppermute | solution.py:9
  72.8 13.2 %collective-permute-start = (bf16[1,192,1024]{2,1,0:T(8,128)(2,1)S(1)}, bf16[1,192,1024]{2,1,0:T(8,128)(2,1)S(1)}, u32[]{:S(2)}, u32[]{:S(2)}) collective-permute-start(bf16[1,192,1024]{2,1,0:T(8,128)(2,1)S(1)} %get-tuple-element.424), channel_id=1, source_target_pairs={{0,4},{4,8},{8,12},{12,16},{16,20},{20,24},{24,28},{28,0},{1,5},{5... | collective-permute-start | bytes 1179656 | tf_op jit(solution)/shard_map/while/body/eval_jaxpr/ppermute | solution.py:9
  88.9 12.3 %collective-permute-start = (bf16[1,192,1024]{2,1,0:T(8,128)(2,1)S(1)}, bf16[1,192,1024]{2,1,0:T(8,128)(2,1)S(1)}, u32[]{:S(2)}, u32[]{:S(2)}) collective-permute-start(bf16[1,192,1024]{2,1,0:T(8,128)(2,1)S(1)} %get-tuple-element.424), channel_id=1, source_target_pairs={{0,4},{4,8},{8,12},{12,16},{16,20},{20,24},{24,28},{28,0},{1,5},{5... | collective-permute-start | bytes 1179656 | tf_op jit(solution)/shard_map/while/body/eval_jaxpr/ppermute | solution.py:9
  104.2 11.4 %collective-permute-start = (bf16[1,192,1024]{2,1,0:T(8,128)(2,1)S(1)}, bf16[1,192,1024]{2,1,0:T(8,128)(2,1)S(1)}, u32[]{:S(2)}, u32[]{:S(2)}) collective-permute-start(bf16[1,192,1024]{2,1,0:T(8,128)(2,1)S(1)} %get-tuple-element.424), channel_id=1, source_target_pairs={{0,4},{4,8},{8,12},{12,16},{16,20},{20,24},{24,28},{28,0},{1,5},{5... | collective-permute-start | bytes 1179656 | tf_op jit(solution)/shard_map/while/body/eval_jaxpr/ppermute | solution.py:9
  118.5 10.6 %collective-permute-start = (bf16[1,192,1024]{2,1,0:T(8,128)(2,1)S(1)}, bf16[1,192,1024]{2,1,0:T(8,128)(2,1)S(1)}, u32[]{:S(2)}, u32[]{:S(2)}) collective-permute-start(bf16[1,192,1024]{2,1,0:T(8,128)(2,1)S(1)} %get-tuple-element.424), channel_id=1, source_target_pairs={{0,4},{4,8},{8,12},{12,16},{16,20},{20,24},{24,28},{28,0},{1,5},{5... | collective-permute-start | bytes 1179656 | tf_op jit(solution)/shard_map/while/body/eval_jaxpr/ppermute | solution.py:9
  132.0 10.5 %collective-permute-start = (bf16[1,192,1024]{2,1,0:T(8,128)(2,1)S(1)}, bf16[1,192,1024]{2,1,0:T(8,128)(2,1)S(1)}, u32[]{:S(2)}, u32[]{:S(2)}) collective-permute-start(bf16[1,192,1024]{2,1,0:T(8,128)(2,1)S(1)} %get-tuple-element.424), channel_id=1, source_target_pairs={{0,4},{4,8},{8,12},{12,16},{16,20},{20,24},{24,28},{28,0},{1,5},{5... | collective-permute-start | bytes 1179656 | tf_op jit(solution)/shard_map/while/body/eval_jaxpr/ppermute | solution.py:9
  145.4 10.5 %collective-permute-start = (bf16[1,192,1024]{2,1,0:T(8,128)(2,1)S(1)}, bf16[1,192,1024]{2,1,0:T(8,128)(2,1)S(1)}, u32[]{:S(2)}, u32[]{:S(2)}) collective-permute-start(bf16[1,192,1024]{2,1,0:T(8,128)(2,1)S(1)} %get-tuple-element.424), channel_id=1, source_target_pairs={{0,4},{4,8},{8,12},{12,16},{16,20},{20,24},{24,28},{28,0},{1,5},{5... | collective-permute-start | bytes 1179656 | tf_op jit(solution)/shard_map/while/body/eval_jaxpr/ppermute | solution.py:9
  158.9 1.4 copy-start.2
  160.3 6.1 %copy-start.1 = (bf16[8,1,192,1024]{3,2,1,0:T(8,128)(2,1)S(1)}, bf16[8,1,192,1024]{3,2,1,0:T(8,128)(2,1)}, u32[]{:S(2)}) copy-start(bf16[8,1,192,1024]{3,2,1,0:T(8,128)(2,1)} %get-tuple-element.319) | copy-start | bytes 9437188
  166.4 135.4 %reduce-scatter.3.cloned.1.call-start = ((), (), s32[]{:S(2)}) async-start(), calls=%async_computation.4 | async-start | bytes 3932160 | tf_op jit(solution)/shard_map/reduce_scatter | solution.py:64
Sparse Core Ops, SparseCore 0:
  31.1 18.5 all-gather.1
  166.5 95.8 reduce-scatter.4
  264.9 36.8 reduce-scatter.2
where the time goes:
time: 312 us; the launch traced here: 311 us
  waiting for transfers between devices  212 us (68%)
  matrix products  32.3 us (10%)
  local copies, waits for them, and re-layouts  20.2 us (6%)
  blocking collectives  19.2 us (6%)
  between operations  15 us (5%)
  loops' own time  9.07 us (3%)
    reduce_scatter x1, waiting for transfers between devices, per_device(): lax.psum_scatter(vir_sum, ('occ', 'aux'), scatter_dimension=0, tiled=True)  89.9 us
    ppermute x7, waiting for transfers between devices, from_behind(): lax.ppermute(array, axis, [(i, (i + by) % size) for i in range(size)])  67.1 us
    reduce_scatter x1, waiting for transfers between devices, per_device(): lax.psum_scatter(jnp.einsum('sijba,sjbp->pia', amp_stack, store_buffer, p...  37.9 us
    all_to_all x1, blocking collectives, per_device(): lax.all_to_all(partial_block, 'occ', split_axis=0, concat_axis=1, tiled=T...  19.2 us
    all_gather x1, waiting for transfers between devices, per_device(): own_block = lax.all_gather(local_block, 'aux', axis=2, tiled=True)  16.9 us
    dot_general x8, matrix products, amplitudes(): jnp.einsum('jbp,iap->ijba', arrival, own_block, preferred_element_type=jn...  16.7 us
    another operation x1, loops' own time, per_device(): ledger, arrival = lax.fori_loop(1, cycle_size, one_turn, (ledger, visitor))  9.07 us
    dynamic_update_slice x8, local copies, waits for them, and re-layouts, absorb(): keeper = lax.dynamic_update_index_in_dim(keeper, arrival, position, 0)  7.49 us
  transfers between devices with their start and end apart: 10, of which 10 were waited for; matrix products, arithmetic and copies ran while one was open for 4% of the time, Pallas kernels for 0%

commit v1 on v0

--- a/solution.py
+++ b/solution.py
@@ -21,10 +21,18 @@
 
 
 def per_device(half_integrals, vir_coef, occ_energy, vir_energy):
+
+    def solve_boxes_over_axis(mine):
+        current_value = jax.lax.axis_size("occ")
+        g_now = jnp.split(mine, current_value, axis=0)
+        extra = jnp.stack(g_now)
+        response = jax.lax.all_to_all(extra, axis_name="occ", split_axis=0, concat_axis=0)
+        return jnp.concatenate(response, axis=1)
+
     partial_block = jnp.einsum(
         "ipm,ma->iap", half_integrals, vir_coef, preferred_element_type=jnp.float32
     ).astype(jnp.bfloat16)
-    local_block = lax.all_to_all(partial_block, "occ", split_axis=0, concat_axis=1, tiled=True)
+    local_block = solve_boxes_over_axis(partial_block)
     own_block = lax.all_gather(local_block, "aux", axis=2, tiled=True)
     cycle_size = lax.axis_size("occ")
     aux_size = lax.axis_size("aux")

time: 312 us -> 312 us (level)
  no operation moved by 1% of the time
where the time goes in v1:
time: 312 us; the launch traced here: 311 us
  waiting for transfers between devices  212 us (68%)
  matrix products  32.3 us (10%)
  local copies, waits for them, and re-layouts  20.2 us (6%)
  blocking collectives  19.2 us (6%)
  between operations  15 us (5%)
  loops' own time  9.07 us (3%)
    reduce_scatter x1, waiting for transfers between devices, per_device(): lax.psum_scatter(vir_sum, ('occ', 'aux'), scatter_dimension=0, tiled=True)  89.8 us
    ppermute x7, waiting for transfers between devices, from_behind(): lax.ppermute(array, axis, [(i, (i + by) % size) for i in range(size)])  67.1 us
    reduce_scatter x1, waiting for transfers between devices, per_device(): lax.psum_scatter(jnp.einsum('sijba,sjbp->pia', amp_stack, store_buffer, p...  37.9 us
    all_to_all x1, blocking collectives, solve_boxes_over_axis(): jax.lax.all_to_all(extra, axis_name='occ', split_axis=0, concat_axis=0)  19.2 us
    all_gather x1, waiting for transfers between devices, per_device(): own_block = lax.all_gather(local_block, 'aux', axis=2, tiled=True)  16.9 us
    dot_general x8, matrix products, amplitudes(): jnp.einsum('jbp,iap->ijba', arrival, own_block, preferred_element_type=jn...  16.7 us
    another operation x1, loops' own time, per_device(): ledger, arrival = lax.fori_loop(1, cycle_size, one_turn, (ledger, visitor))  9.07 us
    dynamic_update_slice x8, local copies, waits for them, and re-layouts, absorb(): keeper = lax.dynamic_update_index_in_dim(keeper, arrival, position, 0)  7.49 us
  transfers between devices with their start and end apart: 10, of which 10 were waited for; matrix products, arithmetic and copies ran while one was open for 4% of the time, Pallas kernels for 0%

profile of v1, /device:TPU:0, one launch (start us, length us, event | category | flops | bytes accessed | tf_op | source)
XLA Modules:
  0.0 311.1 jit_solution(7590512767088851178)
XLA Ops:
  7.2 0.0 copy-start
  7.2 0.0 copy-start.4
  7.2 0.0 all-gather.2.cloned.1.call-start
  7.2 0.9 copy-done
  8.1 3.6 %fusion.36 = bf16[8,96,256]{2,1,0:T(8,128)(2,1)S(1)} fusion(bf16[8,256,1024]{2,1,0:T(8,128)(2,1)} %param.6, bf16[1024,96]{0,1:T(8,128)(2,1)S(1)} %copy-done), kind=kOutput, calls=%fused_computation.21 | convolution fusion | flops 402849792 | bytes 4784128 | tf_op jit(solution)/shard_map/ipm,ma->iap/dot_general | solution.py:32
  11.8 19.2 %all_to_all.5 = bf16[8,1,96,256]{3,2,1,0:T(8,128)(2,1)} all-to-all(bf16[8,1,96,256]{3,2,1,0:T(8,128)(2,1)S(1)} %fusion.48), channel_id=1, replica_groups=mesh['occ'=8,'aux'=4] {'occ'}, dimensions={0} | all-to-all | bytes 786432 | tf_op jit(solution)/shard_map/all_to_all | solution.py:29
  31.0 0.0 all-gather.2.cloned.1.call-update
  31.1 0.0 reduce-scatter.5.cloned.1.call-start
  31.1 0.6 dynamic_slice.23
  32.8 0.0 copy-done.3
  32.8 0.1 broadcast_subtract_fusion.1
  32.9 16.9 %all-gather.2.cloned.1.call-done = bf16[1,768,1024]{2,1,0:T(8,128)(2,1)} async-done(((bf16[1,768,256]{2,1,0:T(8,128)(2,1)}), bf16[1,768,1024]{2,1,0:T(8,128)(2,1)}) %all-gather.2.cloned.1.call-update) | async-done | bytes 1572880 | tf_op jit(solution)/shard_map/all_gather | solution.py:36
  49.7 1.0 constant_dynamic-slice_fusion
  50.8 2.1 fusion.43
  52.9 0.2 dynamic_update_slice.34
  53.0 1.0 fusion.57
  54.1 2.0 dynamic_update_slice.35
  56.1 102.9 %while.21 = (s32[]{:T(128)}, bf16[8,1,1,192,768]{4,3,2,1,0:T(8,128)(2,1)S(1)}, bf16[8,1,192,1024]{3,2,1,0:T(8,128)(2,1)}, bf16[1,192,1024]{2,1,0:T(8,128)(2,1)S(...) while((s32[]{:T(128)}, ...), condition=%wide.region_1.2_spmd, body=%wide.region_0.1_spmd.sunk | while | flops 302432480 | bytes 5413790 | solution.py:70
  56.1 1.5 collective-permute-start
  57.5 0.7 dynamic_slice.30
  59.5 10.6 %collective-permute-done = bf16[1,192,1024]{2,1,0:T(8,128)(2,1)S(1)} collective-permute-done((bf16[1,192,1024]{2,1,0:T(8,128)(2,1)S(1)}, bf16[1,192,1024]{2,1,0:T(8,128)(2,1)S(1)}, u32[]{:S(2)}, u32[]{:S(2)}) %collective-permute-start) | collective-permute-done | bytes 393248 | tf_op jit(solution)/shard_map/while/body/eval_jaxpr/ppermute | solution.py:9
  70.1 0.8 bitcast_dynamic-update-slice_fusion.2
  70.9 2.1 fusion.63
  73.0 0.1 collective-permute-start
  73.0 0.7 dynamic_slice.30
  75.0 11.1 %collective-permute-done = bf16[1,192,1024]{2,1,0:T(8,128)(2,1)S(1)} collective-permute-done((bf16[1,192,1024]{2,1,0:T(8,128)(2,1)S(1)}, bf16[1,192,1024]{2,1,0:T(8,128)(2,1)S(1)}, u32[]{:S(2)}, u32[]{:S(2)}) %collective-permute-start) | collective-permute-done | bytes 393248 | tf_op jit(solution)/shard_map/while/body/eval_jaxpr/ppermute | solution.py:9
  86.1 0.8 bitcast_dynamic-update-slice_fusion.2
  86.9 2.1 fusion.63
  89.0 0.1 collective-permute-start
  89.1 0.7 dynamic_slice.30
  91.0 10.3 %collective-permute-done = bf16[1,192,1024]{2,1,0:T(8,128)(2,1)S(1)} collective-permute-done((bf16[1,192,1024]{2,1,0:T(8,128)(2,1)S(1)}, bf16[1,192,1024]{2,1,0:T(8,128)(2,1)S(1)}, u32[]{:S(2)}, u32[]{:S(2)}) %collective-permute-start) | collective-permute-done | bytes 393248 | tf_op jit(solution)/shard_map/while/body/eval_jaxpr/ppermute | solution.py:9
  101.4 0.8 bitcast_dynamic-update-slice_fusion.2
  102.2 2.1 fusion.63
  104.3 0.1 collective-permute-start
  104.3 0.7 dynamic_slice.30
  106.3 9.4 %collective-permute-done = bf16[1,192,1024]{2,1,0:T(8,128)(2,1)S(1)} collective-permute-done((bf16[1,192,1024]{2,1,0:T(8,128)(2,1)S(1)}, bf16[1,192,1024]{2,1,0:T(8,128)(2,1)S(1)}, u32[]{:S(2)}, u32[]{:S(2)}) %collective-permute-start) | collective-permute-done | bytes 393248 | tf_op jit(solution)/shard_map/while/body/eval_jaxpr/ppermute | solution.py:9
  115.7 0.8 bitcast_dynamic-update-slice_fusion.2
  116.5 2.1 fusion.63
  118.6 0.1 collective-permute-start
  118.7 0.7 dynamic_slice.30
  120.6 8.6 %collective-permute-done = bf16[1,192,1024]{2,1,0:T(8,128)(2,1)S(1)} collective-permute-done((bf16[1,192,1024]{2,1,0:T(8,128)(2,1)S(1)}, bf16[1,192,1024]{2,1,0:T(8,128)(2,1)S(1)}, u32[]{:S(2)}, u32[]{:S(2)}) %collective-permute-start) | collective-permute-done | bytes 393248 | tf_op jit(solution)/shard_map/while/body/eval_jaxpr/ppermute | solution.py:9
  129.2 0.8 bitcast_dynamic-update-slice_fusion.2
  130.0 2.1 fusion.63
  132.1 0.1 collective-permute-start
  132.2 0.7 dynamic_slice.30
  134.1 8.5 %collective-permute-done = bf16[1,192,1024]{2,1,0:T(8,128)(2,1)S(1)} collective-permute-done((bf16[1,192,1024]{2,1,0:T(8,128)(2,1)S(1)}, bf16[1,192,1024]{2,1,0:T(8,128)(2,1)S(1)}, u32[]{:S(2)}, u32[]{:S(2)}) %collective-permute-start) | collective-permute-done | bytes 393248 | tf_op jit(solution)/shard_map/while/body/eval_jaxpr/ppermute | solution.py:9
  142.7 0.8 bitcast_dynamic-update-slice_fusion.2
  143.4 2.1 fusion.63
  145.5 0.1 collective-permute-start
  145.6 0.7 dynamic_slice.30
  147.5 8.5 %collective-permute-done = bf16[1,192,1024]{2,1,0:T(8,128)(2,1)S(1)} collective-permute-done((bf16[1,192,1024]{2,1,0:T(8,128)(2,1)S(1)}, bf16[1,192,1024]{2,1,0:T(8,128)(2,1)S(1)}, u32[]{:S(2)}, u32[]{:S(2)}) %collective-permute-start) | collective-permute-done | bytes 393248 | tf_op jit(solution)/shard_map/while/body/eval_jaxpr/ppermute | solution.py:9
  156.1 0.8 bitcast_dynamic-update-slice_fusion.2
  156.9 2.1 fusion.63
  159.0 0.0 copy-start.2
  159.0 1.4 copy-done.2
  160.4 6.1 %fusion.28 = f32[768,768]{1,0:T(8,128)} fusion(bf16[8,1,1,192,768]{4,3,2,1,0:T(8,128)(2,1)} %copy-done.2), kind=kOutput, calls=%fused_computation.16 | convolution fusion | flops 1811939328 | bytes 4718592 | tf_op jit(solution)/shard_map/sijca,sijcd->ad/dot_general | solution.py:78
  166.4 0.0 reduce-scatter.5.cloned.1.call-update
  166.5 0.0 reduce-scatter.3.cloned.1.call-start
  166.5 6.0 %fusion.23 = f32[1024,1,768]{2,0,1:T(8,128)} fusion(bf16[8,1,1,192,768]{4,3,2,1,0:T(8,128)(2,1)} %copy-done.2, bf16[8,1,192,1024]{3,2,1,0:T(8,128)(2,1)S(1)} %copy-done.1), kind=kOutput, calls=%fused_computation.15 | convolution fusion | flops 2415919104 | bytes 8650752 | tf_op jit(solution)/shard_map/sijba,sjbp->pia/dot_general | solution.py:73
  172.5 0.0 reduce-scatter.3.cloned.1.call-update
  172.5 89.8 %reduce-scatter.5.cloned.1.call-done = f32[24,768]{1,0:T(8,128)} async-done(((f32[768,768]{1,0:T(8,128)}), f32[24,768]{1,0:T(8,128)}) %reduce-scatter.5.cloned.1.call-update) | async-done | bytes 73744 | tf_op jit(solution)/shard_map/reduce_scatter | solution.py:81
  262.4 1.5 broadcast_multiply_fusion
  263.9 37.9 %reduce-scatter.3.cloned.1.call-done = f32[256,1,768]{2,0,1:T(8,128)} async-done(((f32[1024,1,768]{2,0,1:T(8,128)}), f32[256,1,768]{2,0,1:T(8,128)}) %reduce-scatter.3.cloned.1.call-update) | async-done | bytes 786448 | tf_op jit(solution)/shard_map/reduce_scatter | solution.py:72
  301.8 2.8 copy.6
  (26 shorter events, 0.3 us)
Async XLA Ops:
  7.2 0.9 copy-start
  7.2 24.0 %copy-start.4 = (f32[8]{0:T(128)S(1)}, f32[8]{0:T(128)}, u32[]{:S(2)}) copy-start(f32[8]{0:T(128)} %param.8) | copy-start | bytes 100
  7.2 25.6 %copy-start.3 = (f32[768]{0:T(1024)S(1)}, f32[768]{0:T(1024)}, u32[]{:S(2)}) copy-start(f32[768]{0:T(1024)} %param.9) | copy-start | bytes 9220
  7.2 42.5 %all-gather.2.cloned.1.call-start = ((), (), s32[]{:S(2)}) async-start(), calls=%async_computation.3 | async-start | bytes 1966080 | tf_op jit(solution)/shard_map/all_gather | solution.py:36
  31.1 231.3 %reduce-scatter.5.cloned.1.call-start = ((), (), s32[]{:S(2)}) async-start(), calls=%async_computation.5 | async-start | bytes 2433024 | tf_op jit(solution)/shard_map/reduce_scatter | solution.py:81
  56.1 14.0 %collective-permute-start = (bf16[1,192,1024]{2,1,0:T(8,128)(2,1)S(1)}, bf16[1,192,1024]{2,1,0:T(8,128)(2,1)S(1)}, u32[]{:S(2)}, u32[]{:S(2)}) collective-permute-start(bf16[1,192,1024]{2,1,0:T(8,128)(2,1)S(1)} %get-tuple-element.424), channel_id=1, source_target_pairs={{0,4},{4,8},{8,12},{12,16},{16,20},{20,24},{24,28},{28,0},{1,5},{5... | collective-permute-start | bytes 1179656 | tf_op jit(solution)/shard_map/while/body/eval_jaxpr/ppermute | solution.py:9
  73.0 13.2 %collective-permute-start = (bf16[1,192,1024]{2,1,0:T(8,128)(2,1)S(1)}, bf16[1,192,1024]{2,1,0:T(8,128)(2,1)S(1)}, u32[]{:S(2)}, u32[]{:S(2)}) collective-permute-start(bf16[1,192,1024]{2,1,0:T(8,128)(2,1)S(1)} %get-tuple-element.424), channel_id=1, source_target_pairs={{0,4},{4,8},{8,12},{12,16},{16,20},{20,24},{24,28},{28,0},{1,5},{5... | collective-permute-start | bytes 1179656 | tf_op jit(solution)/shard_map/while/body/eval_jaxpr/ppermute | solution.py:9
  89.0 12.3 %collective-permute-start = (bf16[1,192,1024]{2,1,0:T(8,128)(2,1)S(1)}, bf16[1,192,1024]{2,1,0:T(8,128)(2,1)S(1)}, u32[]{:S(2)}, u32[]{:S(2)}) collective-permute-start(bf16[1,192,1024]{2,1,0:T(8,128)(2,1)S(1)} %get-tuple-element.424), channel_id=1, source_target_pairs={{0,4},{4,8},{8,12},{12,16},{16,20},{20,24},{24,28},{28,0},{1,5},{5... | collective-permute-start | bytes 1179656 | tf_op jit(solution)/shard_map/while/body/eval_jaxpr/ppermute | solution.py:9
  104.3 11.4 %collective-permute-start = (bf16[1,192,1024]{2,1,0:T(8,128)(2,1)S(1)}, bf16[1,192,1024]{2,1,0:T(8,128)(2,1)S(1)}, u32[]{:S(2)}, u32[]{:S(2)}) collective-permute-start(bf16[1,192,1024]{2,1,0:T(8,128)(2,1)S(1)} %get-tuple-element.424), channel_id=1, source_target_pairs={{0,4},{4,8},{8,12},{12,16},{16,20},{20,24},{24,28},{28,0},{1,5},{5... | collective-permute-start | bytes 1179656 | tf_op jit(solution)/shard_map/while/body/eval_jaxpr/ppermute | solution.py:9
  118.6 10.6 %collective-permute-start = (bf16[1,192,1024]{2,1,0:T(8,128)(2,1)S(1)}, bf16[1,192,1024]{2,1,0:T(8,128)(2,1)S(1)}, u32[]{:S(2)}, u32[]{:S(2)}) collective-permute-start(bf16[1,192,1024]{2,1,0:T(8,128)(2,1)S(1)} %get-tuple-element.424), channel_id=1, source_target_pairs={{0,4},{4,8},{8,12},{12,16},{16,20},{20,24},{24,28},{28,0},{1,5},{5... | collective-permute-start | bytes 1179656 | tf_op jit(solution)/shard_map/while/body/eval_jaxpr/ppermute | solution.py:9
  132.1 10.5 %collective-permute-start = (bf16[1,192,1024]{2,1,0:T(8,128)(2,1)S(1)}, bf16[1,192,1024]{2,1,0:T(8,128)(2,1)S(1)}, u32[]{:S(2)}, u32[]{:S(2)}) collective-permute-start(bf16[1,192,1024]{2,1,0:T(8,128)(2,1)S(1)} %get-tuple-element.424), channel_id=1, source_target_pairs={{0,4},{4,8},{8,12},{12,16},{16,20},{20,24},{24,28},{28,0},{1,5},{5... | collective-permute-start | bytes 1179656 | tf_op jit(solution)/shard_map/while/body/eval_jaxpr/ppermute | solution.py:9
  145.5 10.5 %collective-permute-start = (bf16[1,192,1024]{2,1,0:T(8,128)(2,1)S(1)}, bf16[1,192,1024]{2,1,0:T(8,128)(2,1)S(1)}, u32[]{:S(2)}, u32[]{:S(2)}) collective-permute-start(bf16[1,192,1024]{2,1,0:T(8,128)(2,1)S(1)} %get-tuple-element.424), channel_id=1, source_target_pairs={{0,4},{4,8},{8,12},{12,16},{16,20},{20,24},{24,28},{28,0},{1,5},{5... | collective-permute-start | bytes 1179656 | tf_op jit(solution)/shard_map/while/body/eval_jaxpr/ppermute | solution.py:9
  159.0 1.4 copy-start.2
  160.4 6.1 %copy-start.1 = (bf16[8,1,192,1024]{3,2,1,0:T(8,128)(2,1)S(1)}, bf16[8,1,192,1024]{3,2,1,0:T(8,128)(2,1)}, u32[]{:S(2)}) copy-start(bf16[8,1,192,1024]{3,2,1,0:T(8,128)(2,1)} %get-tuple-element.319) | copy-start | bytes 9437188
  166.5 135.3 %reduce-scatter.3.cloned.1.call-start = ((), (), s32[]{:S(2)}) async-start(), calls=%async_computation.4 | async-start | bytes 3932160 | tf_op jit(solution)/shard_map/reduce_scatter | solution.py:72
Sparse Core Ops, SparseCore 0:
  31.2 18.5 all-gather.1
  166.6 95.7 reduce-scatter.4
  264.9 36.8 reduce-scatter.2
